TPU v7x, 32 devices: a whole 2x2x4 slice. The times are simulated.
32 devices in a mesh: dp: 4 (over x, core), label: 8 (over z, y).
Axes of the slice: x: 2, y: 2, z: 4, core: 2. Of those that a mesh axis runs over, the one named last changes fastest.
Arguments:
- features: bfloat16 [8192, 768], P(('dp', 'label')), may hold values from -6 to 6
- head_targets: int32 [8192, 4], P(('dp', 'label')), may hold values from 0 to 255
- tail_labels: int32 [8192, 16], P(('dp', 'label')), may hold values from 0 to 1023, as said below
- tail_positive: int32 [8192, 16], P(('dp', 'label')), may hold values 0 or 1
- slots: int32 [32, 8, 128], P(('dp', 'label')), may hold values from 0 to 255, as said below
- counts: int32 [32, 8], P(('dp', 'label')), may hold values from 0 to 128, as said below
- head_weight: float32 [256, 768], P('label'), may hold values from -0.21875 to 0.21875
- head_first: float32 [256, 768], P('label'), may hold values from -0.03125 to 0.03125
- head_second: float32 [256, 768], P('label'), may hold values from 1e-07 to 2e-05
- tail_weight: float32 [1024, 768], P('label'), may hold values from -0.21875 to 0.21875
- tail_first: float32 [1024, 768], P('label'), may hold values from -0.0014648438 to 0.0014648438
- tail_second: float32 [1024, 768], P('label'), may hold values from 1e-09 to 2e-07
Outputs:
- feature_grad: bfloat16 [8192, 768], P(('dp', 'label'))
- head_weight_new: float32 [256, 768], P('label')
- head_first_new: float32 [256, 768], P('label')
- head_second_new: float32 [256, 768], P('label')
- tail_weight_new: float32 [1024, 768], P('label')
- tail_first_new: float32 [1024, 768], P('label')
- tail_second_new: float32 [1024, 768], P('label')
Inputs may be any that keep to these rules, and one draw needn't show every extreme that they name: `tail_labels`: an instance's 16 tail labels form 2 groups of 8 in a row; the labels of a group are distinct and all lie at one owner (label id // 128), and the 2 owners of an instance differ. For s < counts[b, o], slots[b, o, s] lists without repeats the local indices of the instances of block b that have tail labels at owner o, each such instance exactly once; entries beyond the count are arbitrary local indices. The counts of one block sum to 512; in every block some owner has exactly 128, and the blocks b with equal b // 8 give 128 to the same owner.
All inputs are finite; a program needn't handle non-finite values. No bound on the sum of `tail_positive` on one device may be relied on, other than what follows from the above.
Results may differ from a plain program's by a relative error of at most 0.015.
Values may be sent and summed in bfloat16 or wider, within the bound.
No kernel may reach another device: no remote copies, remote signals or barrier semaphores. Data moves between devices by JAX's collectives and lax.ppermute only.
A program may use at most 64 MiB of HBM per device.

v0:
```python
import functools

import jax
import jax.numpy as jnp
from jax import lax
from jax.experimental import pallas as pl
from jax.experimental.pallas import tpu as pltpu
from jax.sharding import PartitionSpec as P

GROUPS = 2
K = 8
ADAM_STEP = 10


def adam_update(weight, first_moment, second, gradient):
    correct_first = 1.0 - 0.9**ADAM_STEP
    correct_second = 1.0 - 0.95**ADAM_STEP
    first_new = 0.9 * first_moment + 0.1 * gradient
    second_new = 0.95 * second + 0.05 * gradient * gradient
    weight_new = weight - 0.003 * (first_new / correct_first) / (
        jnp.sqrt(second_new / correct_second) + 1e-08
    )
    return (weight_new, first_new, second_new)


def flip(value, axis, bits):
    size = lax.axis_size(axis)
    return lax.ppermute(value, axis, [(i, i ^ bits) for i in range(size)])


def gather_dp(value):
    size = lax.axis_size("dp")
    parts = {0: value}
    bit = size // 2
    while bit:
        for k, v in list(parts.items()):
            parts[k | bit] = flip(v, "dp", bit)
        bit //= 2
    return [parts[k] for k in range(size)]


def gather_label(value):
    size = lax.axis_size("label")
    parts = [value] + [flip(value, "label", k) for k in range(2, size, 2)]
    out = []
    for part in parts:
        out += [part, flip(part, "label", 1)]
    return out


def slot_order(owners):
    far = list(range(owners - 1, 0, -2))
    return far + [k - 1 for k in far]


def index_rows(tail_local, labels_ref, positive_ref, targets_ref, slots_ref, counts, out_ref):
    f32, bf16 = jnp.float32, jnp.bfloat16
    short, tok = labels_ref.shape
    positives = targets_ref.shape[0]
    owners, width = slots_ref.shape
    labels = labels_ref[...]
    here = lax.broadcasted_iota(jnp.int32, (tok, width), 0)
    lane = lax.broadcasted_iota(jnp.int32, (1, width), 1)
    row = lax.broadcasted_iota(jnp.int32, (owners, width), 0)
    presence = jnp.zeros((owners, tok), f32)
    for o in range(owners):
        key = jnp.where(lane < counts[0, o], slots_ref[o : o + 1, :], -1)
        match = jnp.where(here == key, 1.0, 0.0).astype(bf16)
        pick = jnp.where(row == o, 1.0, 0.0).astype(bf16)
        presence += lax.dot_general(
            pick, match, (((1,), (1,)), ((), ())), preferred_element_type=f32
        )
    owner_row = lax.broadcasted_iota(jnp.int32, (owners, tok), 0)
    out_ref[:short, :] = labels
    out_ref[short : 2 * short, :] = positive_ref[...]
    last = jnp.zeros((out_ref.shape[0] - 2 * short, tok), jnp.int32)
    at = lax.broadcasted_iota(jnp.int32, last.shape, 0)
    for h in range(positives):
        last = jnp.where(at == h, targets_ref[h : h + 1, :], last)
    for g in range(GROUPS):
        mine = owner_row == labels[g * K : g * K + 1, :] // tail_local
        weight = jnp.sum(jnp.where(mine, presence, 0.0), axis=0, keepdims=True)
        last = jnp.where(at == positives + g, weight.astype(jnp.int32), last)
    out_ref[2 * short :, :] = last


def prep_kernel(tail_local, tq, hq, cut, *refs):
    sources = refs[:7]
    own_ref, info_ref = refs[7:9]
    buffers, sems = refs[9:16], refs[16]
    at_dp = lax.axis_index("dp")
    views = list(sources)
    if cut:
        views[0] = views[0].at[pl.ds(pl.multiple_of(at_dp * tq, tq), tq), :]
        views[1] = views[1].at[pl.ds(pl.multiple_of(at_dp * hq, hq), hq), :]
    copies = [
        pltpu.make_async_copy(view, buffer, sems.at[i])
        for i, (view, buffer) in enumerate(zip(views, buffers))
    ]
    for copy in copies:
        copy.start()
    for copy in copies:
        copy.wait()
    own_ref[:tq, :] = buffers[0][...].astype(jnp.bfloat16)
    own_ref[tq:, :] = buffers[1][...].astype(jnp.bfloat16)
    index_rows(tail_local, *buffers[2:6], buffers[6], info_ref)


def mask_kernel(short, positives, tail_local, head_local, tq, hq, owners, *refs):
    f32, bf16 = jnp.float32, jnp.bfloat16
    infos, (base_ref, sub_ref) = refs[:-2], refs[-2:]
    tok = infos[0].shape[1]
    at_dp = lax.axis_index("dp")
    at_label = lax.axis_index("label")
    column = lax.broadcasted_iota(jnp.int32, (hq, 128), 0)
    head_row = at_dp * hq + column
    tail_row = at_dp * tq + lax.broadcasted_iota(jnp.int32, (tq, 128), 0)
    piece = tq + hq
    for block, info_ref in enumerate(infos):
        for c in range(0, tok, 128):
            lanes = slice(c, c + 128)
            out = slice(block * tok + c, block * tok + c + 128)
            group_owner, hits, takes = [], [], []
            for g in range(GROUPS):
                first = info_ref[g * K : g * K + 1, lanes]
                owner = first // tail_local
                state = jnp.zeros((tq, 128), jnp.int32)
                for s in range(g * K, (g + 1) * K):
                    within = info_ref[s : s + 1, lanes] - owner * tail_local
                    value = 1 + info_ref[short + s : short + s + 1, lanes]
                    state = jnp.where(tail_row == within, value, state)
                at = 2 * short + positives + g
                weight = info_ref[at : at + 1, lanes].astype(f32)
                group_owner.append(owner)
                hits.append(jnp.where(state > 0, weight, 0.0))
                takes.append(jnp.where(state > 1, weight, 0.0))
            for place, k in enumerate(slot_order(owners)):
                owner = at_label ^ k
                rows = slice(place * piece, place * piece + tq)
                base = jnp.zeros((tq, 128), f32)
                sub = jnp.zeros((tq, 128), f32)
                for g in range(GROUPS):
                    mine = group_owner[g] == owner
                    base = jnp.where(mine, hits[g], base)
                    sub = jnp.where(mine, takes[g], sub)
                base_ref[rows, out] = base.astype(bf16)
                sub_ref[rows, out] = sub.astype(bf16)
                target = jnp.zeros((hq, 128), f32)
                for h in range(positives):
                    at = 2 * short + h
                    within = info_ref[at : at + 1, lanes] - owner * head_local
                    target = jnp.where(within == head_row, 1.0, target)
                rows = slice(place * piece + tq, (place + 1) * piece)
                base_ref[rows, out] = jnp.ones((hq, 128), bf16)
                sub_ref[rows, out] = target.astype(bf16)


def adam_kernel(token_total, tq, hq, *refs):
    states, outs = refs[-12:-6], refs[-6:]
    at_dp = lax.axis_index("dp")
    for k, piece_ref in enumerate(refs[:-12]):
        at = at_dp ^ k
        for first, count, column in ((0, hq, tq), (3, tq, 0)):
            rows = pl.ds(pl.multiple_of(at * count, count), count)
            gradient = piece_ref[column : column + count, :].astype(jnp.float32) / token_total
            new = adam_update(*(ref[rows, :] for ref in states[first : first + 3]), gradient)
            for ref, value in zip(outs[first : first + 3], new):
                ref[rows, :] = value


def in_dp_order(parts):
    at_dp = lax.axis_index("dp")
    size = len(parts)
    bit = 1
    while bit < size:
        odd = (at_dp & bit) != 0
        parts = [jnp.where(odd, parts[k ^ bit], parts[k]) for k in range(size)]
        bit *= 2
    return parts


def on_device(
    features,
    head_targets,
    tail_labels,
    tail_positive,
    slots,
    counts,
    head_weight,
    head_first,
    head_second,
    tail_weight,
    tail_first,
    tail_second,
):
    tok, width = features.shape
    owners = lax.axis_size("label")
    replicas = lax.axis_size("dp")
    at_dp = lax.axis_index("dp")
    tail_local = tail_weight.shape[0]
    head_local = head_weight.shape[0]
    token_total = tok * owners * replicas
    short = tail_labels.shape[1]
    positives = head_targets.shape[1]
    f32, bf16 = jnp.float32, jnp.bfloat16
    tq, hq = tail_local // replicas, head_local // replicas
    piece = tq + hq
    vmem = pl.BlockSpec(memory_space=pltpu.VMEM)

    feats = jnp.concatenate(gather_dp(features))

    info_rows = -(-(2 * short + positives + GROUPS) // 8) * 8
    cut = hq % 8 == 0 and tq % 16 == 0
    share = (tail_weight, head_weight)
    if not cut:
        share = (
            lax.dynamic_slice_in_dim(tail_weight, at_dp * tq, tq),
            lax.dynamic_slice_in_dim(head_weight, at_dp * hq, hq),
        )
    prep = pl.pallas_call(
        functools.partial(prep_kernel, tail_local, tq, hq, cut),
        out_shape=(
            jax.ShapeDtypeStruct((piece, width), bf16),
            jax.ShapeDtypeStruct((info_rows, tok), jnp.int32),
        ),
        in_specs=[pl.BlockSpec(memory_space=pltpu.HBM)] * 7,
        out_specs=(vmem, vmem),
        scratch_shapes=[
            pltpu.VMEM((tq, width), f32),
            pltpu.VMEM((hq, width), f32),
            pltpu.VMEM((short, tok), jnp.int32),
            pltpu.VMEM((short, tok), jnp.int32),
            pltpu.VMEM((positives, tok), jnp.int32),
            pltpu.VMEM(slots.shape[1:], jnp.int32),
            pltpu.SMEM(counts.shape, jnp.int32),
            pltpu.SemaphoreType.DMA((7,)),
        ],
        name="prep",
    )
    own, info = prep(
        *share, tail_labels.T, tail_positive.T, head_targets.T, slots[0], counts
    )
    pieces = gather_label(own)
    rows = jnp.concatenate([pieces[k] for k in slot_order(owners)])
    infos = gather_dp(info)
    masks = jax.ShapeDtypeStruct((owners * piece, replicas * tok), bf16)
    base, sub = pl.pallas_call(
        functools.partial(
            mask_kernel, short, positives, tail_local, head_local, tq, hq, owners
        ),
        out_shape=(masks, masks),
        in_specs=[vmem] * replicas,
        out_specs=(vmem, vmem),
        compiler_params=pltpu.CompilerParams(vmem_limit_bytes=16 << 20),
        name="mask",
    )(*infos)

    logits = lax.dot_general(rows, feats, (((1,), (1,)), ((), ())), preferred_element_type=f32)
    coef = (base.astype(f32) * jax.nn.sigmoid(logits) - sub.astype(f32)).astype(bf16)
    grad = jnp.dot(coef, feats, preferred_element_type=f32).astype(bf16)
    part = lax.dot_general(
        coef, rows, (((0,), (0,)), ((), ())), preferred_element_type=f32
    ).astype(bf16)
    part = part.reshape(replicas, tok, width)

    half = owners // 2 * piece
    cuts = (0, owners // 4 * piece, half)
    sums = []
    for lo, hi in zip(cuts, cuts[1:]):
        got = flip(grad[lo:hi], "label", 1)
        sums.append(grad[half + lo : half + hi].astype(f32) + got.astype(f32))
    sums = jnp.concatenate(sums)
    steps = slot_order(owners)[owners // 2 :]
    total = sums[-piece:]
    for n, k in enumerate(steps[:-1]):
        got = flip(sums[n * piece : (n + 1) * piece].astype(bf16), "label", k)
        total = total + got.astype(f32)
    done = gather_dp(total.astype(bf16))

    bit = 1
    sums = [part[k] for k in range(replicas)]
    while bit < replicas:
        got = [flip(sums[k + 1], "dp", bit) for k in range(0, len(sums), 2)]
        sums = [sums[2 * j].astype(f32) + got[j].astype(f32) for j in range(len(got))]
        bit *= 2
        if bit < replicas:
            sums = [sums[0]] + [v.astype(bf16) for v in sums[1:]]
    feature_grad = sums[0].astype(bf16)

    states = (head_weight, head_first, head_second, tail_weight, tail_first, tail_second)
    if cut:
        new = pl.pallas_call(
            functools.partial(adam_kernel, token_total, tq, hq),
            out_shape=tuple(jax.ShapeDtypeStruct(v.shape, v.dtype) for v in states),
            in_specs=[vmem] * (replicas + 6),
            out_specs=(vmem,) * 6,
            compiler_params=pltpu.CompilerParams(vmem_limit_bytes=12 << 20),
            name="adam",
        )(*done, *states)
    else:
        done = in_dp_order(done)
        tail_gradient = jnp.concatenate([p[:tq] for p in done]).astype(f32) / token_total
        head_gradient = jnp.concatenate([p[tq:] for p in done]).astype(f32) / token_total
        new = adam_update(*states[:3], head_gradient) + adam_update(*states[3:], tail_gradient)
    return (feature_grad, *new)


def solution(mesh):
    split = P(("dp", "label"), None)
    rows = P("label", None)
    in_specs = (split,) * 4 + (P(("dp", "label"), None, None), split) + (rows,) * 6
    out_specs = (split,) + (rows,) * 6
    return jax.shard_map(
        on_device, mesh=mesh, in_specs=in_specs, out_specs=out_specs, check_vma=False
    )
```

profile of v0, /device:TPU:0, one launch (start us, length us, event | category | flops | bytes accessed | tf_op | source)
XLA Modules:
  0.0 58.2 jit_solution(7977413878668016340)
XLA Ops:
  0.6 1.9 %prep.1 = (bf16[40,768]{1,0:T(8,128)(2,1)}, s32[40,256]{1,0:T(8,128)}) custom-call(f32[128,768]{1,0:T(8,128)} %refs_7_.1, f32[32,768]{1,0:T(8,128)} %refs_4_.1, s32[16,256]{1,0:T(8,128)} %bitcast.10, s32[16,256]{1,0:T(8,128)} %bitcast.11, s32[4,256]{1,0:T(4,128)} %bitcast.12, s32[8,128]{1,0:T(8,128)} %bitcast.13, s32[1,8]{1,0:T(1,128)} %refs_6_.2), custom_call_target="tpu_custom_call" | custom-call | tf_op jit(solution)/shard_map/prep/pallas_call | solution.py:240
  2.5 5.1 %collective-permute-start.3 = (bf16[40,768]{1,0:T(8,128)(2,1)}, bf16[40,768]{1,0:T(8,128)(2,1)S(1)}, u32[]{:S(2)}, u32[]{:S(2)}) collective-permute-start(bf16[40,768]{1,0:T(8,128)(2,1)} %get-tuple-element.19), channel_id=1, source_target_pairs={{0,6},{1,7},{2,4},{3,5},{4,2},{5,3},{6,0},{7,1},{8,14},{9,15},{10,... | collective-permute-start | bytes 184328 | tf_op jit(solution)/shard_map/ppermute | solution.py:28
  7.7 1.5 %collective-permute-start.1 = (s32[40,256]{1,0:T(8,128)}, s32[40,256]{1,0:T(8,128)S(1)}, u32[]{:S(2)}, u32[]{:S(2)}) collective-permute-start(s32[40,256]{1,0:T(8,128)} %get-tuple-element.17.refs_0_), channel_id=1, source_target_pairs={{0,16},{8,24},{16,0},{24,8},{1,17},{9,25},{17,1},{25,9},{2,18},{10... | collective-permute-start | bytes 122888 | tf_op jit(solution)/shard_map/ppermute | solution.py:28
  9.9 1.9 %collective-permute-done.1.refs_2_ = s32[40,256]{1,0:T(8,128)S(1)} collective-permute-done((s32[40,256]{1,0:T(8,128)}, s32[40,256]{1,0:T(8,128)S(1)}, u32[]{:S(2)}, u32[]{:S(2)}) %collective-permute-start.1) | collective-permute-done | bytes 40992 | tf_op jit(solution)/shard_map/ppermute | solution.py:28
  11.9 1.5 %collective-permute-start.4 = (bf16[40,768]{1,0:T(8,128)(2,1)S(1)}, bf16[40,768]{1,0:T(8,128)(2,1)S(1)}, u32[]{:S(2)}, u32[]{:S(2)}) collective-permute-start(bf16[40,768]{1,0:T(8,128)(2,1)S(1)} %collective-permute-done.3), channel_id=1, source_target_pairs={{0,1},{1,0},{2,3},{3,2},{4,5},{5,4},{6,7},{7,6},{8,9},{9,8},{10,11... | collective-permute-start | bytes 184328 | tf_op jit(solution)/shard_map/ppermute | solution.py:28
  13.4 1.0 %constant_dynamic-update-slice_fusion.11 = bf16[1024,768]{1,0:T(8,128)(2,1)S(1)} fusion(bf16[256,768]{1,0:T(8,128)(2,1)} %param.12), kind=kLoop, calls=%fused_computation.27 | loop fusion | bytes 786432
  15.0 1.5 %collective-permute-start.11 = (bf16[256,768]{1,0:T(8,128)(2,1)}, bf16[256,768]{1,0:T(8,128)(2,1)S(1)}, u32[]{:S(2)}, u32[]{:S(2)}) collective-permute-start(bf16[256,768]{1,0:T(8,128)(2,1)} %param.12), channel_id=1, source_target_pairs={{0,16},{8,24},{16,0},{24,8},{1,17},{9,25},{17,1},{25,9},{2,18},{10... | collective-permute-start | bytes 1179656 | tf_op jit(solution)/shard_map/ppermute | solution.py:28
  18.1 1.6 %collective-permute-start.6 = (bf16[40,768]{1,0:T(8,128)(2,1)S(1)}, bf16[40,768]{1,0:T(8,128)(2,1)S(1)}, u32[]{:S(2)}, u32[]{:S(2)}) collective-permute-start(bf16[40,768]{1,0:T(8,128)(2,1)S(1)} %collective-permute-done.5), channel_id=1, source_target_pairs={{0,1},{1,0},{2,3},{3,2},{4,5},{5,4},{6,7},{7,6},{8,9},{9,8},{10,11... | collective-permute-start | bytes 184328 | tf_op jit(solution)/shard_map/ppermute | solution.py:28
  20.2 2.4 %collective-permute-done.6 = bf16[40,768]{1,0:T(8,128)(2,1)S(1)} collective-permute-done((bf16[40,768]{1,0:T(8,128)(2,1)S(1)}, bf16[40,768]{1,0:T(8,128)(2,1)S(1)}, u32[]{:S(2)}, u32[]{:S(2)}) %collective-permute-start.6) | collective-permute-done | bytes 61472 | tf_op jit(solution)/shard_map/ppermute | solution.py:28
  22.5 1.3 %collective-permute-done.8 = bf16[40,768]{1,0:T(8,128)(2,1)S(1)} collective-permute-done((bf16[40,768]{1,0:T(8,128)(2,1)S(1)}, bf16[40,768]{1,0:T(8,128)(2,1)S(1)}, u32[]{:S(2)}, u32[]{:S(2)}) %collective-permute-start.8) | collective-permute-done | bytes 61472 | tf_op jit(solution)/shard_map/ppermute | solution.py:28
  23.9 2.3 %collective-permute-done.11 = bf16[256,768]{1,0:T(8,128)(2,1)S(1)} collective-permute-done((bf16[256,768]{1,0:T(8,128)(2,1)}, bf16[256,768]{1,0:T(8,128)(2,1)S(1)}, u32[]{:S(2)}, u32[]{:S(2)}) %collective-permute-start.11) | collective-permute-done | bytes 393248 | tf_op jit(solution)/shard_map/ppermute | solution.py:28
  26.3 1.6 %collective-permute-done.12 = bf16[256,768]{1,0:T(8,128)(2,1)S(1)} collective-permute-done((bf16[256,768]{1,0:T(8,128)(2,1)S(1)}, bf16[256,768]{1,0:T(8,128)(2,1)S(1)}, u32[]{:S(2)}, u32[]{:S(2)}) %collective-permute-start.12) | collective-permute-done | bytes 393248 | tf_op jit(solution)/shard_map/ppermute | solution.py:28
  29.8 1.0 %convolution_convert_fusion = bf16[1024,768]{1,0:T(8,128)(2,1)S(1)} fusion(bf16[320,1024]{1,0:T(8,128)(2,1)S(1)} %subtract_convert_fusion, bf16[320,768]{1,0:T(8,128)(2,1)S(1)} %constant_dynamic-update-slice_fusion), kind=kOutput, calls=%fused_computation | convolution fusion | flops 504102912 | bytes 2719744 | tf_op jit(solution)/shard_map/dot_general | solution.py:261
  30.8 1.6 %collective-permute-start.16 = (bf16[80,768]{1,0:T(8,128)(2,1)S(1)}, bf16[80,768]{1,0:T(8,128)(2,1)S(1)}, u32[]{:S(2)}, u32[]{:S(2)}) collective-permute-start(bf16[80,768]{1,0:T(8,128)(2,1)S(1)} %get-tuple-element.32), channel_id=1, source_target_pairs={{0,1},{1,0},{2,3},{3,2},{4,5},{5,4},{6,7},{7,6},{8,9},{9,8},{10,11... | collective-permute-start | bytes 368648 | tf_op jit(solution)/shard_map/ppermute | solution.py:28
  33.6 3.5 %collective-permute-done.16 = bf16[80,768]{1,0:T(8,128)(2,1)S(1)} collective-permute-done((bf16[80,768]{1,0:T(8,128)(2,1)S(1)}, bf16[80,768]{1,0:T(8,128)(2,1)S(1)}, u32[]{:S(2)}, u32[]{:S(2)}) %collective-permute-start.16) | collective-permute-done | bytes 122912 | tf_op jit(solution)/shard_map/ppermute | solution.py:28
  37.1 1.8 %collective-permute-done.17 = bf16[80,768]{1,0:T(8,128)(2,1)S(1)} collective-permute-done((bf16[80,768]{1,0:T(8,128)(2,1)S(1)}, bf16[80,768]{1,0:T(8,128)(2,1)S(1)}, u32[]{:S(2)}, u32[]{:S(2)}) %collective-permute-start.17) | collective-permute-done | bytes 122912 | tf_op jit(solution)/shard_map/ppermute | solution.py:28
  39.0 1.8 %collective-permute-start.18 = (bf16[40,768]{1,0:T(8,128)(2,1)S(1)}, bf16[40,768]{1,0:T(8,128)(2,1)S(1)}, u32[]{:S(2)}, u32[]{:S(2)}) collective-permute-start(bf16[40,768]{1,0:T(8,128)(2,1)S(1)} %get-tuple-element.33), channel_id=1, source_target_pairs={{0,6},{1,7},{2,4},{3,5},{4,2},{5,3},{6,0},{7,1},{8,14},{9,15},{10,... | collective-permute-start | bytes 184328 | tf_op jit(solution)/shard_map/ppermute | solution.py:28
  40.8 2.7 %collective-permute-start.20 = (bf16[40,768]{1,0:T(8,128)(2,1)S(1)}, bf16[40,768]{1,0:T(8,128)(2,1)S(1)}, u32[]{:S(2)}, u32[]{:S(2)}) collective-permute-start(bf16[40,768]{1,0:T(8,128)(2,1)S(1)} %slice.79), channel_id=1, source_target_pairs={{0,2},{1,3},{2,0},{3,1},{4,6},{5,7},{6,4},{7,5},{8,10},{9,11},{10,... | collective-permute-start | bytes 184328 | tf_op jit(solution)/shard_map/ppermute | solution.py:28
  43.6 1.6 %collective-permute-start.15 = (bf16[256,768]{1,0:T(8,128)(2,1)S(1)}, bf16[256,768]{1,0:T(8,128)(2,1)S(1)}, u32[]{:S(2)}, u32[]{:S(2)}) collective-permute-start(bf16[256,768]{1,0:T(8,128)(2,1)S(1)} %add_convert_fusion.1), channel_id=1, source_target_pairs={{0,16},{8,24},{16,0},{24,8},{1,17},{9,25},{17,1},{25,9},{2,18},{10... | collective-permute-start | bytes 1179656 | tf_op jit(solution)/shard_map/ppermute | solution.py:28
  45.6 1.1 %collective-permute-done.19 = bf16[40,768]{1,0:T(8,128)(2,1)S(1)} collective-permute-done((bf16[40,768]{1,0:T(8,128)(2,1)S(1)}, bf16[40,768]{1,0:T(8,128)(2,1)S(1)}, u32[]{:S(2)}, u32[]{:S(2)}) %collective-permute-start.19) | collective-permute-done | bytes 61472 | tf_op jit(solution)/shard_map/ppermute | solution.py:28
  46.8 1.1 %collective-permute-start.22 = (bf16[40,768]{1,0:T(8,128)(2,1)S(1)}, bf16[40,768]{1,0:T(8,128)(2,1)S(1)}, u32[]{:S(2)}, u32[]{:S(2)}) collective-permute-start(bf16[40,768]{1,0:T(8,128)(2,1)S(1)} %fusion.5.refs_0_), channel_id=1, source_target_pairs={{0,16},{8,24},{16,0},{24,8},{1,17},{9,25},{17,1},{25,9},{2,18},{10... | collective-permute-start | bytes 184328 | tf_op jit(solution)/shard_map/ppermute | solution.py:28
  47.9 6.6 %collective-permute-done.22.refs_2_ = bf16[40,768]{1,0:T(8,128)(2,1)S(1)} collective-permute-done((bf16[40,768]{1,0:T(8,128)(2,1)S(1)}, bf16[40,768]{1,0:T(8,128)(2,1)S(1)}, u32[]{:S(2)}, u32[]{:S(2)}) %collective-permute-start.22) | collective-permute-done | bytes 61472 | tf_op jit(solution)/shard_map/ppermute | solution.py:28
  54.4 1.2 %collective-permute-done.23.refs_3_ = bf16[40,768]{1,0:T(8,128)(2,1)S(1)} collective-permute-done((bf16[40,768]{1,0:T(8,128)(2,1)S(1)}, bf16[40,768]{1,0:T(8,128)(2,1)S(1)}, u32[]{:S(2)}, u32[]{:S(2)}) %collective-permute-start.23) | collective-permute-done | bytes 61472 | tf_op jit(solution)/shard_map/ppermute | solution.py:28
  55.7 1.6 %adam.1 = (f32[32,768]{1,0:T(8,128)}, f32[32,768]{1,0:T(8,128)}, f32[32,768]{1,0:T(8,128)}, f32[128,768]{1,0:T(8,128)}, f32[128,768]{1,0:T(8,128)}, /*index=5*/f32[128,768]{1,0:T(8,128)}) custom-call(bf16[40,768]{1,0:T(8,128)(2,1)S(1)} %fusion.5.refs_0_, bf16[40,768]{1,0:T(8,128)(2,1)S(1)} %collective-permute-done.21.refs_1_, ...), custom_call_target="tpu_custom_call" | custom-call | tf_op jit(solution)/shard_map/adam/pallas_call | solution.py:292
  (67 shorter events, 8.1 us)
Async XLA Ops:
  2.5 9.4 %collective-permute-start.3 = (bf16[40,768]{1,0:T(8,128)(2,1)}, bf16[40,768]{1,0:T(8,128)(2,1)S(1)}, u32[]{:S(2)}, u32[]{:S(2)}) collective-permute-start(bf16[40,768]{1,0:T(8,128)(2,1)} %get-tuple-element.19), channel_id=1, source_target_pairs={{0,6},{1,7},{2,4},{3,5},{4,2},{5,3},{6,0},{7,1},{8,14},{9,15},{10,... | collective-permute-start | bytes 184328 | tf_op jit(solution)/shard_map/ppermute | solution.py:28
  7.7 4.2 %collective-permute-start.1 = (s32[40,256]{1,0:T(8,128)}, s32[40,256]{1,0:T(8,128)S(1)}, u32[]{:S(2)}, u32[]{:S(2)}) collective-permute-start(s32[40,256]{1,0:T(8,128)} %get-tuple-element.17.refs_0_), channel_id=1, source_target_pairs={{0,16},{8,24},{16,0},{24,8},{1,17},{9,25},{17,1},{25,9},{2,18},{10... | collective-permute-start | bytes 122888 | tf_op jit(solution)/shard_map/ppermute | solution.py:28
  9.2 8.8 %collective-permute-start.5 = (bf16[40,768]{1,0:T(8,128)(2,1)}, bf16[40,768]{1,0:T(8,128)(2,1)S(1)}, u32[]{:S(2)}, u32[]{:S(2)}) collective-permute-start(bf16[40,768]{1,0:T(8,128)(2,1)} %get-tuple-element.19), channel_id=1, source_target_pairs={{0,4},{1,5},{2,6},{3,7},{4,0},{5,1},{6,2},{7,3},{8,12},{9,13},{10,... | collective-permute-start | bytes 184328 | tf_op jit(solution)/shard_map/ppermute | solution.py:28
  9.2 8.9 %collective-permute-start.7 = (bf16[40,768]{1,0:T(8,128)(2,1)}, bf16[40,768]{1,0:T(8,128)(2,1)S(1)}, u32[]{:S(2)}, u32[]{:S(2)}) collective-permute-start(bf16[40,768]{1,0:T(8,128)(2,1)} %get-tuple-element.19), channel_id=1, source_target_pairs={{0,2},{1,3},{2,0},{3,1},{4,6},{5,7},{6,4},{7,5},{8,10},{9,11},{10,... | collective-permute-start | bytes 184328 | tf_op jit(solution)/shard_map/ppermute | solution.py:28
  9.9 4.5 %collective-permute-start = (s32[40,256]{1,0:T(8,128)}, s32[40,256]{1,0:T(8,128)S(1)}, u32[]{:S(2)}, u32[]{:S(2)}) collective-permute-start(s32[40,256]{1,0:T(8,128)} %get-tuple-element.17.refs_0_), channel_id=1, source_target_pairs={{0,8},{8,0},{16,24},{24,16},{1,9},{9,1},{17,25},{25,17},{2,10},{10... | collective-permute-start | bytes 122888 | tf_op jit(solution)/shard_map/ppermute | solution.py:28
  11.9 3.1 %collective-permute-start.2 = (s32[40,256]{1,0:T(8,128)S(1)}, s32[40,256]{1,0:T(8,128)S(1)}, u32[]{:S(2)}, u32[]{:S(2)}) collective-permute-start(s32[40,256]{1,0:T(8,128)S(1)} %collective-permute-done.1.refs_2_), channel_id=1, source_target_pairs={{0,8},{8,0},{16,24},{24,16},{1,9},{9,1},{17,25},{25,17},{2,10},{10... | collective-permute-start | bytes 122888 | tf_op jit(solution)/shard_map/ppermute | solution.py:28
  11.9 7.8 %collective-permute-start.4 = (bf16[40,768]{1,0:T(8,128)(2,1)S(1)}, bf16[40,768]{1,0:T(8,128)(2,1)S(1)}, u32[]{:S(2)}, u32[]{:S(2)}) collective-permute-start(bf16[40,768]{1,0:T(8,128)(2,1)S(1)} %collective-permute-done.3), channel_id=1, source_target_pairs={{0,1},{1,0},{2,3},{3,2},{4,5},{5,4},{6,7},{7,6},{8,9},{9,8},{10,11... | collective-permute-start | bytes 184328 | tf_op jit(solution)/shard_map/ppermute | solution.py:28
  14.4 9.4 %collective-permute-start.9 = (bf16[40,768]{1,0:T(8,128)(2,1)}, bf16[40,768]{1,0:T(8,128)(2,1)S(1)}, u32[]{:S(2)}, u32[]{:S(2)}) collective-permute-start(bf16[40,768]{1,0:T(8,128)(2,1)} %get-tuple-element.19), channel_id=1, source_target_pairs={{0,1},{1,0},{2,3},{3,2},{4,5},{5,4},{6,7},{7,6},{8,9},{9,8},{10,11... | collective-permute-start | bytes 184328 | tf_op jit(solution)/shard_map/ppermute | solution.py:28
  15.0 11.2 %collective-permute-start.11 = (bf16[256,768]{1,0:T(8,128)(2,1)}, bf16[256,768]{1,0:T(8,128)(2,1)S(1)}, u32[]{:S(2)}, u32[]{:S(2)}) collective-permute-start(bf16[256,768]{1,0:T(8,128)(2,1)} %param.12), channel_id=1, source_target_pairs={{0,16},{8,24},{16,0},{24,8},{1,17},{9,25},{17,1},{25,9},{2,18},{10... | collective-permute-start | bytes 1179656 | tf_op jit(solution)/shard_map/ppermute | solution.py:28
  18.0 8.3 %collective-permute-start.10 = (bf16[256,768]{1,0:T(8,128)(2,1)}, bf16[256,768]{1,0:T(8,128)(2,1)S(1)}, u32[]{:S(2)}, u32[]{:S(2)}) collective-permute-start(bf16[256,768]{1,0:T(8,128)(2,1)} %param.12), channel_id=1, source_target_pairs={{0,8},{8,0},{16,24},{24,16},{1,9},{9,1},{17,25},{25,17},{2,10},{10... | collective-permute-start | bytes 1179656 | tf_op jit(solution)/shard_map/ppermute | solution.py:28
  18.1 4.5 %collective-permute-start.6 = (bf16[40,768]{1,0:T(8,128)(2,1)S(1)}, bf16[40,768]{1,0:T(8,128)(2,1)S(1)}, u32[]{:S(2)}, u32[]{:S(2)}) collective-permute-start(bf16[40,768]{1,0:T(8,128)(2,1)S(1)} %collective-permute-done.5), channel_id=1, source_target_pairs={{0,1},{1,0},{2,3},{3,2},{4,5},{5,4},{6,7},{7,6},{8,9},{9,8},{10,11... | collective-permute-start | bytes 184328 | tf_op jit(solution)/shard_map/ppermute | solution.py:28
  19.6 4.2 %collective-permute-start.8 = (bf16[40,768]{1,0:T(8,128)(2,1)S(1)}, bf16[40,768]{1,0:T(8,128)(2,1)S(1)}, u32[]{:S(2)}, u32[]{:S(2)}) collective-permute-start(bf16[40,768]{1,0:T(8,128)(2,1)S(1)} %collective-permute-done.7), channel_id=1, source_target_pairs={{0,1},{1,0},{2,3},{3,2},{4,5},{5,4},{6,7},{7,6},{8,9},{9,8},{10,11... | collective-permute-start | bytes 184328 | tf_op jit(solution)/shard_map/ppermute | solution.py:28
  26.2 1.7 %collective-permute-start.12 = (bf16[256,768]{1,0:T(8,128)(2,1)S(1)}, bf16[256,768]{1,0:T(8,128)(2,1)S(1)}, u32[]{:S(2)}, u32[]{:S(2)}) collective-permute-start(bf16[256,768]{1,0:T(8,128)(2,1)S(1)} %collective-permute-done.11), channel_id=1, source_target_pairs={{0,8},{8,0},{16,24},{24,16},{1,9},{9,1},{17,25},{25,17},{2,10},{10... | collective-permute-start | bytes 1179656 | tf_op jit(solution)/shard_map/ppermute | solution.py:28
  30.8 6.3 %collective-permute-start.16 = (bf16[80,768]{1,0:T(8,128)(2,1)S(1)}, bf16[80,768]{1,0:T(8,128)(2,1)S(1)}, u32[]{:S(2)}, u32[]{:S(2)}) collective-permute-start(bf16[80,768]{1,0:T(8,128)(2,1)S(1)} %get-tuple-element.32), channel_id=1, source_target_pairs={{0,1},{1,0},{2,3},{3,2},{4,5},{5,4},{6,7},{7,6},{8,9},{9,8},{10,11... | collective-permute-start | bytes 368648 | tf_op jit(solution)/shard_map/ppermute | solution.py:28
  32.4 6.5 %collective-permute-start.17 = (bf16[80,768]{1,0:T(8,128)(2,1)S(1)}, bf16[80,768]{1,0:T(8,128)(2,1)S(1)}, u32[]{:S(2)}, u32[]{:S(2)}) collective-permute-start(bf16[80,768]{1,0:T(8,128)(2,1)S(1)} %get-tuple-element.31), channel_id=1, source_target_pairs={{0,1},{1,0},{2,3},{3,2},{4,5},{5,4},{6,7},{7,6},{8,9},{9,8},{10,11... | collective-permute-start | bytes 368648 | tf_op jit(solution)/shard_map/ppermute | solution.py:28
  33.0 10.5 %collective-permute-start.14 = (bf16[256,768]{1,0:T(8,128)(2,1)S(1)}, bf16[256,768]{1,0:T(8,128)(2,1)S(1)}, u32[]{:S(2)}, u32[]{:S(2)}) collective-permute-start(bf16[256,768]{1,0:T(8,128)(2,1)S(1)} %get-tuple-element.28), channel_id=1, source_target_pairs={{0,8},{8,0},{16,24},{24,16},{1,9},{9,1},{17,25},{25,17},{2,10},{10... | collective-permute-start | bytes 1179656 | tf_op jit(solution)/shard_map/ppermute | solution.py:28
  33.1 24.2 %collective-permute-start.13 = (bf16[256,768]{1,0:T(8,128)(2,1)S(1)}, bf16[256,768]{1,0:T(8,128)(2,1)S(1)}, u32[]{:S(2)}, u32[]{:S(2)}) collective-permute-start(bf16[256,768]{1,0:T(8,128)(2,1)S(1)} %get-tuple-element.27), channel_id=1, source_target_pairs={{0,8},{8,0},{16,24},{24,16},{1,9},{9,1},{17,25},{25,17},{2,10},{10... | collective-permute-start | bytes 1179656 | tf_op jit(solution)/shard_map/ppermute | solution.py:28
  39.0 6.6 %collective-permute-start.18 = (bf16[40,768]{1,0:T(8,128)(2,1)S(1)}, bf16[40,768]{1,0:T(8,128)(2,1)S(1)}, u32[]{:S(2)}, u32[]{:S(2)}) collective-permute-start(bf16[40,768]{1,0:T(8,128)(2,1)S(1)} %get-tuple-element.33), channel_id=1, source_target_pairs={{0,6},{1,7},{2,4},{3,5},{4,2},{5,3},{6,0},{7,1},{8,14},{9,15},{10,... | collective-permute-start | bytes 184328 | tf_op jit(solution)/shard_map/ppermute | solution.py:28
  40.8 5.9 %collective-permute-start.19 = (bf16[40,768]{1,0:T(8,128)(2,1)S(1)}, bf16[40,768]{1,0:T(8,128)(2,1)S(1)}, u32[]{:S(2)}, u32[]{:S(2)}) collective-permute-start(bf16[40,768]{1,0:T(8,128)(2,1)S(1)} %get-tuple-element.34), channel_id=1, source_target_pairs={{0,4},{1,5},{2,6},{3,7},{4,0},{5,1},{6,2},{7,3},{8,12},{9,13},{10,... | collective-permute-start | bytes 184328 | tf_op jit(solution)/shard_map/ppermute | solution.py:28
  40.8 5.9 %collective-permute-start.20 = (bf16[40,768]{1,0:T(8,128)(2,1)S(1)}, bf16[40,768]{1,0:T(8,128)(2,1)S(1)}, u32[]{:S(2)}, u32[]{:S(2)}) collective-permute-start(bf16[40,768]{1,0:T(8,128)(2,1)S(1)} %slice.79), channel_id=1, source_target_pairs={{0,2},{1,3},{2,0},{3,1},{4,6},{5,7},{6,4},{7,5},{8,10},{9,11},{10,... | collective-permute-start | bytes 184328 | tf_op jit(solution)/shard_map/ppermute | solution.py:28
  43.6 13.7 %collective-permute-start.15 = (bf16[256,768]{1,0:T(8,128)(2,1)S(1)}, bf16[256,768]{1,0:T(8,128)(2,1)S(1)}, u32[]{:S(2)}, u32[]{:S(2)}) collective-permute-start(bf16[256,768]{1,0:T(8,128)(2,1)S(1)} %add_convert_fusion.1), channel_id=1, source_target_pairs={{0,16},{8,24},{16,0},{24,8},{1,17},{9,25},{17,1},{25,9},{2,18},{10... | collective-permute-start | bytes 1179656 | tf_op jit(solution)/shard_map/ppermute | solution.py:28
  46.8 7.7 %collective-permute-start.22 = (bf16[40,768]{1,0:T(8,128)(2,1)S(1)}, bf16[40,768]{1,0:T(8,128)(2,1)S(1)}, u32[]{:S(2)}, u32[]{:S(2)}) collective-permute-start(bf16[40,768]{1,0:T(8,128)(2,1)S(1)} %fusion.5.refs_0_), channel_id=1, source_target_pairs={{0,16},{8,24},{16,0},{24,8},{1,17},{9,25},{17,1},{25,9},{2,18},{10... | collective-permute-start | bytes 184328 | tf_op jit(solution)/shard_map/ppermute | solution.py:28
  47.9 6.6 %collective-permute-start.21 = (bf16[40,768]{1,0:T(8,128)(2,1)S(1)}, bf16[40,768]{1,0:T(8,128)(2,1)S(1)}, u32[]{:S(2)}, u32[]{:S(2)}) collective-permute-start(bf16[40,768]{1,0:T(8,128)(2,1)S(1)} %fusion.5.refs_0_), channel_id=1, source_target_pairs={{0,8},{8,0},{16,24},{24,16},{1,9},{9,1},{17,25},{25,17},{2,10},{10... | collective-permute-start | bytes 184328 | tf_op jit(solution)/shard_map/ppermute | solution.py:28
  54.4 1.2 %collective-permute-start.23 = (bf16[40,768]{1,0:T(8,128)(2,1)S(1)}, bf16[40,768]{1,0:T(8,128)(2,1)S(1)}, u32[]{:S(2)}, u32[]{:S(2)}) collective-permute-start(bf16[40,768]{1,0:T(8,128)(2,1)S(1)} %collective-permute-done.22.refs_2_), channel_id=1, source_target_pairs={{0,8},{8,0},{16,24},{24,16},{1,9},{9,1},{17,25},{25,17},{2,10},{10... | collective-permute-start | bytes 184328 | tf_op jit(solution)/shard_map/ppermute | solution.py:28
  (8 other events, 160.6 us)
where the time goes:
time: 58.4 us; the launch traced here: 58.2 us
  waiting for transfers between devices  24.2 us (41%)
  starting transfers between devices  23 us (39%)
  Pallas kernels  4.08 us (7%)
  matrix products  2.51 us (4%)
  local copies, waits for them, and re-layouts  2.06 us (4%)
  other arithmetic  1.39 us (2%)
  between operations  0.94 us (2%)
    ppermute x24, waiting for transfers between devices, flip(): return lax.ppermute(value, axis, [(i, i ^ bits) for i in range(size)])  24.2 us
    ppermute x24, starting transfers between devices, flip(): return lax.ppermute(value, axis, [(i, i ^ bits) for i in range(size)])  23 us
    unnamed x26, local copies, waits for them, and re-layouts  1.94 us
    pallas_call x1, Pallas kernels, on_device(): prep(*share, tail_labels.T, tail_positive.T, head_targets.T, slots[0], co...  1.87 us
    pallas_call x1, Pallas kernels, on_device(): pl.pallas_call(functools.partial(adam_kernel, token_total, tq, hq), out_s...  1.55 us
  transfers between devices with their start and end apart: 24, of which 11 were waited for; matrix products, arithmetic and copies ran while one was open for 2% of the time, Pallas kernels for 4%

commit v1 on v0

v1 whole, which is shorter than its diff:
```python
import functools

import jax
import jax.numpy as jnp
from jax import lax
from jax.experimental import pallas as pl
from jax.experimental.pallas import tpu as pltpu
from jax.sharding import PartitionSpec as P

GROUPS = 2
K = 8
ADAM_STEP = 10


def adam_update(weight, first_moment, second, gradient):
    correct_first = 1.0 - 0.9**ADAM_STEP
    correct_second = 1.0 - 0.95**ADAM_STEP
    first_new = 0.9 * first_moment + 0.1 * gradient
    second_new = 0.95 * second + 0.05 * gradient * gradient
    weight_new = weight - 0.003 * (first_new / correct_first) / (
        jnp.sqrt(second_new / correct_second) + 1e-08
    )
    return (weight_new, first_new, second_new)


def flip(value, axis, bits):
    size = lax.axis_size(axis)
    return lax.ppermute(value, axis, [(i, i ^ bits) for i in range(size)])


def dp_order(size):
    order, bit = [0], size // 2
    while bit:
        order += [k | bit for k in order]
        bit //= 2
    return order


def gather_dp(value, near=None):
    parts = [value]
    bit = lax.axis_size("dp") // 2
    while bit:
        parts += [flip(v, "dp", bit) for v in parts]
        bit //= 2
    return jnp.concatenate([value if near is None else near] + parts[1:])


def gather_dp_joined(value):
    bit = lax.axis_size("dp") // 2
    while bit:
        value = jnp.concatenate([value, flip(value, "dp", bit)])
        bit //= 2
    return value


def stage_kernel(in_ref, out_ref):
    out_ref[...] = in_ref[...]


def gather_label(value):
    size = lax.axis_size("label")
    parts = [value] + [flip(value, "label", k) for k in range(2, size, 2)]
    out = []
    for part in parts:
        out += [part, flip(part, "label", 1)]
    return out


def slot_order(owners):
    far = list(range(owners - 1, 0, -2))
    return far + [k - 1 for k in far]


def index_lines(short, positives):
    starts, at = [], 0
    for count in (short, short, GROUPS, GROUPS, positives, positives):
        starts.append(at)
        at += count
    return starts, at


def index_values(tail_local, labels_ref, positive_ref, targets_ref, slots_ref, counts):
    f32, bf16 = jnp.float32, jnp.bfloat16
    _, tok = labels_ref.shape
    owners, width = slots_ref.shape
    labels = labels_ref[...]
    here = lax.broadcasted_iota(jnp.int32, (tok, width), 0)
    lane = lax.broadcasted_iota(jnp.int32, (1, width), 1)
    row = lax.broadcasted_iota(jnp.int32, (owners, width), 0)
    presence = jnp.zeros((owners, tok), f32)
    for o in range(owners):
        key = jnp.where(lane < counts[0, o], slots_ref[o : o + 1, :], -1)
        match = jnp.where(here == key, 1.0, 0.0).astype(bf16)
        pick = jnp.where(row == o, 1.0, 0.0).astype(bf16)
        presence += lax.dot_general(
            pick, match, (((1,), (1,)), ((), ())), preferred_element_type=f32
        )
    owner_row = lax.broadcasted_iota(jnp.int32, (owners, tok), 0)
    owner = labels // tail_local
    weights = []
    for g in range(GROUPS):
        mine = owner_row == owner[g * K : g * K + 1, :]
        weights.append(jnp.sum(jnp.where(mine, presence, 0.0), axis=0, keepdims=True))
    targets = targets_ref[...]
    high = targets // 256
    lines = [labels - owner * tail_local, positive_ref[...]]
    lines += [owner[g * K : g * K + 1, :] for g in range(GROUPS)] + weights
    lines += [high, targets - high * 256]
    return [
        line[i : i + 1, :].astype(f32) for line in lines for i in range(line.shape[0])
    ]


def prep_kernel(tail_local, tq, hq, cut, *refs):
    sources = refs[:7]
    own_ref, lines_ref = refs[7:9]
    buffers, sems = refs[9:16], refs[16]
    at_dp = lax.axis_index("dp")
    tok = sources[2].shape[1]
    views = list(sources)
    if cut:
        views[0] = views[0].at[pl.ds(pl.multiple_of(at_dp * tq, tq), tq), :]
        views[1] = views[1].at[pl.ds(pl.multiple_of(at_dp * hq, hq), hq), :]
    copies = [
        pltpu.make_async_copy(view, target, sems.at[i])
        for i, (view, target) in enumerate(zip(views, buffers))
    ]
    for copy in copies:
        copy.start()
    for copy in copies:
        copy.wait()
    own_ref[:tq, :] = buffers[0][...].astype(jnp.bfloat16)
    own_ref[tq:, :] = buffers[1][...].astype(jnp.bfloat16)
    lines = index_values(tail_local, *buffers[2:6], buffers[6])
    count, width = lines_ref.shape
    lines_a_row = width // tok
    at = lax.broadcasted_iota(jnp.int32, (count, tok), 0)
    for lane in range(lines_a_row):
        block = jnp.zeros((count, tok), jnp.float32)
        for row, line in enumerate(lines[lane::lines_a_row]):
            block = jnp.where(at == row, line, block)
        lines_ref[:, lane * tok : (lane + 1) * tok] = block.astype(jnp.bfloat16)


def mask_kernel(short, positives, tq, hq, owners, tok, lines_ref, base_ref, sub_ref):
    f32, bf16 = jnp.float32, jnp.bfloat16
    replicas = base_ref.shape[1] // tok
    count = lines_ref.shape[0] // replicas
    lines_a_row = lines_ref.shape[1] // tok
    starts, _ = index_lines(short, positives)
    at_dp = lax.axis_index("dp")
    at_label = lax.axis_index("label")
    piece = tq + hq
    head_local = hq * replicas
    head_row = (at_dp * hq + lax.broadcasted_iota(jnp.int32, (hq, 128), 0)).astype(f32)
    tail_row = (at_dp * tq + lax.broadcasted_iota(jnp.int32, (tq, 128), 0)).astype(f32)
    for block in range(replicas):
        rows = lines_ref[block * count : (block + 1) * count, :].astype(f32)
        for c in range(0, tok, 128):

            def line(kind, i):
                n = starts[kind] + i
                lane = (n % lines_a_row) * tok + c
                row = n // lines_a_row
                return rows[row : row + 1, lane : lane + 128]

            out = slice(block * tok + c, block * tok + c + 128)
            hits, takes = [], []
            for g in range(GROUPS):
                state = jnp.zeros((tq, 128), f32)
                for s in range(g * K, (g + 1) * K):
                    state = jnp.where(tail_row == line(0, s), 1.0 + line(1, s), state)
                weight = line(3, g)
                hits.append(jnp.where(state > 0.0, weight, 0.0))
                takes.append(jnp.where(state > 1.0, weight, 0.0))
            targets = [256.0 * line(4, h) + line(5, h) for h in range(positives)]
            for place, k in enumerate(slot_order(owners)):
                owner = (at_label ^ k).astype(f32)
                out_rows = slice(place * piece, place * piece + tq)
                base = jnp.zeros((tq, 128), f32)
                sub = jnp.zeros((tq, 128), f32)
                for g in range(GROUPS):
                    mine = line(2, g) == owner
                    base = jnp.where(mine, hits[g], base)
                    sub = jnp.where(mine, takes[g], sub)
                base_ref[out_rows, out] = base.astype(bf16)
                sub_ref[out_rows, out] = sub.astype(bf16)
                target = jnp.zeros((hq, 128), f32)
                for value in targets:
                    target = jnp.where(value - owner * head_local == head_row, 1.0, target)
                out_rows = slice(place * piece + tq, (place + 1) * piece)
                base_ref[out_rows, out] = jnp.ones((hq, 128), bf16)
                sub_ref[out_rows, out] = target.astype(bf16)


def adam_kernel(token_total, tq, hq, replicas, *refs):
    states, outs = refs[-12:-6], refs[-6:]
    at_dp = lax.axis_index("dp")
    pieces = [ref.at[i : i + tq + hq] for ref in refs[:-12] for i in range(0, ref.shape[0], tq + hq)]
    for piece_ref, k in zip(pieces, dp_order(replicas)):
        at = at_dp ^ k
        for first, count, column in ((0, hq, tq), (3, tq, 0)):
            rows = pl.ds(pl.multiple_of(at * count, count), count)
            gradient = piece_ref[column : column + count, :].astype(jnp.float32) / token_total
            new = adam_update(*(ref[rows, :] for ref in states[first : first + 3]), gradient)
            for ref, value in zip(outs[first : first + 3], new):
                ref[rows, :] = value


def in_dp_order(value):
    size = lax.axis_size("dp")
    parts = jnp.split(value, size)
    parts = [parts[dp_order(size).index(k)] for k in range(size)]
    at_dp = lax.axis_index("dp")
    bit = 1
    while bit < size:
        odd = (at_dp & bit) != 0
        parts = [jnp.where(odd, parts[k ^ bit], parts[k]) for k in range(size)]
        bit *= 2
    return parts


def on_device(
    features,
    head_targets,
    tail_labels,
    tail_positive,
    slots,
    counts,
    head_weight,
    head_first,
    head_second,
    tail_weight,
    tail_first,
    tail_second,
):
    tok, width = features.shape
    owners = lax.axis_size("label")
    replicas = lax.axis_size("dp")
    at_dp = lax.axis_index("dp")
    tail_local = tail_weight.shape[0]
    head_local = head_weight.shape[0]
    token_total = tok * owners * replicas
    short = tail_labels.shape[1]
    positives = head_targets.shape[1]
    f32, bf16 = jnp.float32, jnp.bfloat16
    tq, hq = tail_local // replicas, head_local // replicas
    piece = tq + hq
    vmem = pl.BlockSpec(memory_space=pltpu.VMEM)

    lines_a_row = width // tok
    count = -(-index_lines(short, positives)[1] // lines_a_row // 16) * 16
    cut = hq % 8 == 0 and tq % 16 == 0
    share = (tail_weight, head_weight)
    if not cut:
        share = (
            lax.dynamic_slice_in_dim(tail_weight, at_dp * tq, tq),
            lax.dynamic_slice_in_dim(head_weight, at_dp * hq, hq),
        )
    prep = pl.pallas_call(
        functools.partial(prep_kernel, tail_local, tq, hq, cut),
        out_shape=(
            jax.ShapeDtypeStruct((piece, width), bf16),
            jax.ShapeDtypeStruct((count, width), bf16),
        ),
        in_specs=[pl.BlockSpec(memory_space=pltpu.HBM)] * 7,
        out_specs=(vmem, vmem),
        scratch_shapes=[
            pltpu.VMEM((tq, width), f32),
            pltpu.VMEM((hq, width), f32),
            pltpu.VMEM((short, tok), jnp.int32),
            pltpu.VMEM((short, tok), jnp.int32),
            pltpu.VMEM((positives, tok), jnp.int32),
            pltpu.VMEM(slots.shape[1:], jnp.int32),
            pltpu.SMEM(counts.shape, jnp.int32),
            pltpu.SemaphoreType.DMA((7,)),
        ],
        compiler_params=pltpu.CompilerParams(vmem_limit_bytes=4 << 20),
        name="prep",
    )
    sources = (*share, tail_labels.T, tail_positive.T, head_targets.T, slots[0], counts)
    own, mine = prep(
        *(pltpu.with_memory_space_constraint(v, pltpu.HBM) for v in sources)
    )
    pieces = gather_label(own)
    order = slot_order(owners)
    halves = order[: owners // 2], order[owners // 2 :]
    rows_far, rows_near = (jnp.concatenate([pieces[k] for k in half]) for half in halves)

    stage = pl.pallas_call(
        stage_kernel,
        out_shape=jax.ShapeDtypeStruct(features.shape, bf16),
        in_specs=[vmem],
        out_specs=vmem,
        compiler_params=pltpu.CompilerParams(vmem_limit_bytes=4 << 20),
        name="stage",
    )
    near = stage(features)
    feats = gather_dp(features, near)
    lines = gather_dp_joined(mine)
    masks = jax.ShapeDtypeStruct((owners * piece, replicas * tok), bf16)
    masked = pl.pallas_call(
        functools.partial(mask_kernel, short, positives, tq, hq, owners, tok),
        out_shape=(masks, masks),
        in_specs=[vmem],
        out_specs=(vmem, vmem),
        compiler_params=pltpu.CompilerParams(vmem_limit_bytes=16 << 20),
        name="mask",
    )
    base, sub = masked(lines)

    def product(rows, at):
        logits = lax.dot_general(rows, feats, (((1,), (1,)), ((), ())), preferred_element_type=f32)
        own_base, own_sub = (v[at : at + rows.shape[0]].astype(f32) for v in (base, sub))
        coef = (own_base * jax.nn.sigmoid(logits) - own_sub).astype(bf16)
        grad = jnp.dot(coef, feats, preferred_element_type=f32).astype(bf16)
        return coef, grad

    half = owners // 2 * piece
    coef_far, grad_far = product(rows_far, 0)
    rows_near, grad_far = lax.optimization_barrier((rows_near, grad_far))
    coef_near, grad_near = product(rows_near, half)
    coef = jnp.concatenate([coef_far, coef_near])
    rows = jnp.concatenate([rows_far, rows_near])
    cut_at = replicas * tok // 2
    sent = lax.dot_general(
        coef[:, cut_at:], rows, (((0,), (0,)), ((), ())), preferred_element_type=f32
    ).astype(bf16)
    coef, sent = lax.optimization_barrier((coef, sent))
    kept = lax.dot_general(
        coef[:, :cut_at], rows, (((0,), (0,)), ((), ())), preferred_element_type=f32
    ).astype(bf16)
    kept = lax.optimization_barrier(kept)

    cuts = (0, owners // 4 * piece, half)
    sums = []
    for lo, hi in zip(cuts, cuts[1:]):
        got = flip(grad_far[lo:hi], "label", 1)
        if sums:
            got, _ = lax.optimization_barrier((got, sums[0]))
        got = got.astype(f32)
        for at in range(0, hi - lo, piece):
            first = lo + at
            sums.append(grad_near[first : first + piece].astype(f32) + got[at : at + piece])
    total = sums[-1]
    for value, k in zip(sums[:-1], slot_order(owners)[owners // 2 :]):
        total = total + flip(value.astype(bf16), "label", k).astype(f32)
    done = gather_dp_joined(total.astype(bf16))

    bit, part = 1, kept
    while bit < replicas:
        if bit > 1:
            cut_at = part.shape[0] // 2
            part, sent = part[:cut_at], part[cut_at:].astype(bf16)
        got = flip(sent, "dp", bit)
        part = part.astype(f32) + got.astype(f32)
        bit *= 2
    feature_grad = part.astype(bf16)

    states = (head_weight, head_first, head_second, tail_weight, tail_first, tail_second)
    if cut:
        new = pl.pallas_call(
            functools.partial(adam_kernel, token_total, tq, hq, replicas),
            out_shape=tuple(jax.ShapeDtypeStruct(v.shape, v.dtype) for v in states),
            in_specs=[vmem] * 7,
            out_specs=(vmem,) * 6,
            compiler_params=pltpu.CompilerParams(vmem_limit_bytes=12 << 20),
            name="adam",
        )(done, *states)
    else:
        done = in_dp_order(done)
        tail_gradient = jnp.concatenate([p[:tq] for p in done]).astype(f32) / token_total
        head_gradient = jnp.concatenate([p[tq:] for p in done]).astype(f32) / token_total
        new = adam_update(*states[:3], head_gradient) + adam_update(*states[3:], tail_gradient)
    return (feature_grad, *new)


def solution(mesh):
    split = P(("dp", "label"), None)
    rows = P("label", None)
    in_specs = (split,) * 4 + (P(("dp", "label"), None, None), split) + (rows,) * 6
    out_specs = (split,) + (rows,) * 6
    return jax.shard_map(
        on_device, mesh=mesh, in_specs=in_specs, out_specs=out_specs, check_vma=False
    )
```

time: 58.4 us -> 58.7 us (level)
  starting transfers between devices: 23 us -> 25.9 us
  waiting for transfers between devices: 24.2 us -> 22.1 us
  matrix products: 2.51 us -> 3.57 us
  local copies, waits for them, and re-layouts: 2.06 us -> 1.13 us
    ppermute x24 -> x21, starting transfers between devices: 23 us -> 25.9 us  [flip(): return lax.ppermute(value, axis, [(i, i ^ bits) for i in range(size)])]
    ppermute x24 -> x21, waiting for transfers between devices: 24.2 us -> 22.1 us  [flip(): return lax.ppermute(value, axis, [(i, i ^ bits) for i in range(size)])]
    dot_general x3 -> x6, matrix products: 2.51 us -> 3.57 us  [the longest x2 1.48 us: product(): lax.dot_general(rows, feats, (((1,), (1,)), ((), ())), preferred_element_...]
    unnamed x26 -> x18, local copies, waits for them, and re-layouts: 1.94 us -> 1.06 us
    pallas_call x3 -> x4, Pallas kernels: 4.08 us -> 3.51 us  [the longest x1 1.55 us: on_device(): pl.pallas_call(functools.partial(adam_kernel, token_total, tq, hq, replic...]
    convert_element_type x4 -> x5, other arithmetic: 1.33 us -> 0.93 us  [the longest x1 0.81 us: on_device(): feature_grad = part.astype(bf16)]
  transfers between devices with their start and end apart: 24 -> 21, of which waited for: 11 -> 10; matrix products, arithmetic and copies ran while one was open for 2% -> 5% of each run, Pallas kernels for 4% -> 6%
where the time goes in v1:
time: 58.7 us; the launch traced here: 58.5 us
  starting transfers between devices  25.9 us (44%)
  waiting for transfers between devices  22.1 us (38%)
  matrix products  3.57 us (6%)
  Pallas kernels  3.51 us (6%)
  other arithmetic  1.21 us (2%)
  local copies, waits for them, and re-layouts  1.13 us (2%)
  between operations  0.98 us (2%)
    ppermute x21, starting transfers between devices, flip(): return lax.ppermute(value, axis, [(i, i ^ bits) for i in range(size)])  25.9 us
    ppermute x21, waiting for transfers between devices, flip(): return lax.ppermute(value, axis, [(i, i ^ bits) for i in range(size)])  22.1 us
    pallas_call x1, Pallas kernels, on_device(): pl.pallas_call(functools.partial(adam_kernel, token_total, tq, hq, replic...  1.55 us
    dot_general x2, matrix products, product(): lax.dot_general(rows, feats, (((1,), (1,)), ((), ())), preferred_element_...  1.48 us
    pallas_call x1, Pallas kernels, on_device(): prep(*(pltpu.with_memory_space_constraint(v, pltpu.HBM) for v in sources))  1.24 us
  transfers between devices with their start and end apart: 21, of which 10 were waited for; matrix products, arithmetic and copies ran while one was open for 5% of the time, Pallas kernels for 6%

profile of v1, /device:TPU:0, one launch (start us, length us, event | category | flops | bytes accessed | tf_op | source)
XLA Modules:
  0.0 58.5 jit_solution(5571333834891702185)
XLA Ops:
  0.6 3.0 %collective-permute-start.9 = (bf16[256,768]{1,0:T(8,128)(2,1)}, bf16[256,768]{1,0:T(8,128)(2,1)S(1)}, u32[]{:S(2)}, u32[]{:S(2)}) collective-permute-start(bf16[256,768]{1,0:T(8,128)(2,1)} %in_ref.1), channel_id=1, source_target_pairs={{0,16},{8,24},{16,0},{24,8},{1,17},{9,25},{17,1},{25,9},{2,18},{10... | collective-permute-start | bytes 1179656 | tf_op jit(solution)/shard_map/ppermute | solution.py:28
  3.7 1.2 %prep.1 = (bf16[40,768]{1,0:T(8,128)(2,1)S(1)}, bf16[16,768]{1,0:T(8,128)(2,1)S(1)}) custom-call(f32[128,768]{1,0:T(8,128)} %refs_4_.1, f32[32,768]{1,0:T(8,128)} %refs_1_.3, s32[16,256]{1,0:T(8,128)} %bitcast.9, s32[16,256]{1,0:T(8,128)} %bitcast.10, s32[4,256]{1,0:T(4,128)} %bitcast.11, s32[8,128]{1,0:T(8,128)} %bitcast.12, s32[1,8]{1,0:T(1,128)} %refs_6_.2), custom_call_target="tpu_custom_call" | custom-call | tf_op jit(solution)/shard_map/prep/pallas_call | solution.py:282
  5.0 2.0 %collective-permute-start.8 = (bf16[40,768]{1,0:T(8,128)(2,1)S(1)}, bf16[40,768]{1,0:T(8,128)(2,1)S(1)}, u32[]{:S(2)}, u32[]{:S(2)}) collective-permute-start(bf16[40,768]{1,0:T(8,128)(2,1)S(1)} %get-tuple-element.24), channel_id=1, source_target_pairs={{0,1},{1,0},{2,3},{3,2},{4,5},{5,4},{6,7},{7,6},{8,9},{9,8},{10,11... | collective-permute-start | bytes 184328 | tf_op jit(solution)/shard_map/ppermute | solution.py:28
  7.0 1.6 %collective-permute-start.6 = (bf16[40,768]{1,0:T(8,128)(2,1)S(1)}, bf16[40,768]{1,0:T(8,128)(2,1)S(1)}, u32[]{:S(2)}, u32[]{:S(2)}) collective-permute-start(bf16[40,768]{1,0:T(8,128)(2,1)S(1)} %get-tuple-element.24), channel_id=1, source_target_pairs={{0,2},{1,3},{2,0},{3,1},{4,6},{5,7},{6,4},{7,5},{8,10},{9,11},{10,... | collective-permute-start | bytes 184328 | tf_op jit(solution)/shard_map/ppermute | solution.py:28
  8.6 2.6 %collective-permute-start.4 = (bf16[40,768]{1,0:T(8,128)(2,1)S(1)}, bf16[40,768]{1,0:T(8,128)(2,1)S(1)}, u32[]{:S(2)}, u32[]{:S(2)}) collective-permute-start(bf16[40,768]{1,0:T(8,128)(2,1)S(1)} %get-tuple-element.24), channel_id=1, source_target_pairs={{0,4},{1,5},{2,6},{3,7},{4,0},{5,1},{6,2},{7,3},{8,12},{9,13},{10,... | collective-permute-start | bytes 184328 | tf_op jit(solution)/shard_map/ppermute | solution.py:28
  11.2 1.0 %copy-done.1 = bf16[256,768]{1,0:T(8,128)(2,1)S(1)} copy-done((bf16[256,768]{1,0:T(8,128)(2,1)S(1)}, bf16[256,768]{1,0:T(8,128)(2,1)}, u32[]{:S(2)}) %copy-start.1) | copy-done | bytes 393240
  12.2 1.3 %collective-permute-done = bf16[16,768]{1,0:T(8,128)(2,1)S(1)} collective-permute-done((bf16[16,768]{1,0:T(8,128)(2,1)S(1)}, bf16[16,768]{1,0:T(8,128)(2,1)S(1)}, u32[]{:S(2)}, u32[]{:S(2)}) %collective-permute-start) | collective-permute-done | bytes 24608 | tf_op jit(solution)/shard_map/ppermute | solution.py:28
  13.5 3.8 %collective-permute-start.2 = (bf16[40,768]{1,0:T(8,128)(2,1)S(1)}, bf16[40,768]{1,0:T(8,128)(2,1)S(1)}, u32[]{:S(2)}, u32[]{:S(2)}) collective-permute-start(bf16[40,768]{1,0:T(8,128)(2,1)S(1)} %get-tuple-element.24), channel_id=1, source_target_pairs={{0,6},{1,7},{2,4},{3,5},{4,2},{5,3},{6,0},{7,1},{8,14},{9,15},{10,... | collective-permute-start | bytes 184328 | tf_op jit(solution)/shard_map/ppermute | solution.py:28
  18.0 1.7 %collective-permute-done.2 = bf16[40,768]{1,0:T(8,128)(2,1)S(1)} collective-permute-done((bf16[40,768]{1,0:T(8,128)(2,1)S(1)}, bf16[40,768]{1,0:T(8,128)(2,1)S(1)}, u32[]{:S(2)}, u32[]{:S(2)}) %collective-permute-start.2) | collective-permute-done | bytes 61472 | tf_op jit(solution)/shard_map/ppermute | solution.py:28
  19.7 1.6 %collective-permute-start.7 = (bf16[40,768]{1,0:T(8,128)(2,1)S(1)}, bf16[40,768]{1,0:T(8,128)(2,1)S(1)}, u32[]{:S(2)}, u32[]{:S(2)}) collective-permute-start(bf16[40,768]{1,0:T(8,128)(2,1)S(1)} %collective-permute-done.6), channel_id=1, source_target_pairs={{0,1},{1,0},{2,3},{3,2},{4,5},{5,4},{6,7},{7,6},{8,9},{9,8},{10,11... | collective-permute-start | bytes 184328 | tf_op jit(solution)/shard_map/ppermute | solution.py:28
  22.5 3.5 %collective-permute-done.3 = bf16[40,768]{1,0:T(8,128)(2,1)S(1)} collective-permute-done((bf16[40,768]{1,0:T(8,128)(2,1)S(1)}, bf16[40,768]{1,0:T(8,128)(2,1)S(1)}, u32[]{:S(2)}, u32[]{:S(2)}) %collective-permute-start.3) | collective-permute-done | bytes 61472 | tf_op jit(solution)/shard_map/ppermute | solution.py:28
  26.2 4.0 %collective-permute-done.5 = bf16[40,768]{1,0:T(8,128)(2,1)S(1)} collective-permute-done((bf16[40,768]{1,0:T(8,128)(2,1)S(1)}, bf16[40,768]{1,0:T(8,128)(2,1)S(1)}, u32[]{:S(2)}, u32[]{:S(2)}) %collective-permute-start.5) | collective-permute-done | bytes 61472 | tf_op jit(solution)/shard_map/ppermute | solution.py:28
  30.3 0.7 %fusion.11 = bf16[160,1024]{1,0:T(8,128)(2,1)S(1)} fusion(bf16[320,1024]{1,0:T(8,128)(2,1)S(1)} %get-tuple-element.25, bf16[320,1024]{1,0:T(8,128)(2,1)S(1)} %get-tuple-element.23, bf16[40,768]{1,0:T(8,128)(2,1)S(1)} %collective-permute-done.8, bf16[40,768]{1,0:T(8,128)(2,1)S(1)} %collective-permute-done.7, bf16[40,768]{1,0:T(8,128)(2,1)S(1)} %collective-permute-done.5, ...), kind=kOutput, calls=%fused_computation.17 | convolution fusion | flops 260243456 | bytes 2801664 | tf_op jit(solution)/shard_map/dot_general | solution.py:313
  31.8 1.8 %collective-permute-start.14 = (bf16[80,768]{1,0:T(8,128)(2,1)S(1)}, bf16[80,768]{1,0:T(8,128)(2,1)S(1)}, u32[]{:S(2)}, u32[]{:S(2)}) collective-permute-start(bf16[80,768]{1,0:T(8,128)(2,1)S(1)} %get-tuple-element.40), channel_id=1, source_target_pairs={{0,1},{1,0},{2,3},{3,2},{4,5},{5,4},{6,7},{7,6},{8,9},{9,8},{10,11... | collective-permute-start | bytes 368648 | tf_op jit(solution)/shard_map/ppermute | solution.py:28
  35.6 0.9 %collective-permute-done.15 = bf16[80,768]{1,0:T(8,128)(2,1)S(1)} collective-permute-done((bf16[80,768]{1,0:T(8,128)(2,1)S(1)}, bf16[80,768]{1,0:T(8,128)(2,1)S(1)}, u32[]{:S(2)}, u32[]{:S(2)}) %collective-permute-start.15) | collective-permute-done | bytes 122912 | tf_op jit(solution)/shard_map/ppermute | solution.py:28
  36.5 3.7 %collective-permute-start.16 = (bf16[40,768]{1,0:T(8,128)(2,1)S(1)}, bf16[40,768]{1,0:T(8,128)(2,1)S(1)}, u32[]{:S(2)}, u32[]{:S(2)}) collective-permute-start(bf16[40,768]{1,0:T(8,128)(2,1)S(1)} %slice_add_fusion.4), channel_id=1, source_target_pairs={{0,6},{1,7},{2,4},{3,5},{4,2},{5,3},{6,0},{7,1},{8,14},{9,15},{10,... | collective-permute-start | bytes 184328 | tf_op jit(solution)/shard_map/ppermute | solution.py:28
  40.4 1.8 %collective-permute-start.18 = (bf16[40,768]{1,0:T(8,128)(2,1)S(1)}, bf16[40,768]{1,0:T(8,128)(2,1)S(1)}, u32[]{:S(2)}, u32[]{:S(2)}) collective-permute-start(bf16[40,768]{1,0:T(8,128)(2,1)S(1)} %get-tuple-element.38), channel_id=1, source_target_pairs={{0,2},{1,3},{2,0},{3,1},{4,6},{5,7},{6,4},{7,5},{8,10},{9,11},{10,... | collective-permute-start | bytes 184328 | tf_op jit(solution)/shard_map/ppermute | solution.py:28
  42.8 2.7 %collective-permute-done.17 = bf16[40,768]{1,0:T(8,128)(2,1)S(1)} collective-permute-done((bf16[40,768]{1,0:T(8,128)(2,1)S(1)}, bf16[40,768]{1,0:T(8,128)(2,1)S(1)}, u32[]{:S(2)}, u32[]{:S(2)}) %collective-permute-start.17) | collective-permute-done | bytes 61472 | tf_op jit(solution)/shard_map/ppermute | solution.py:28
  45.9 1.6 %collective-permute-start.19 = (bf16[40,768]{1,0:T(8,128)(2,1)S(1)}, bf16[40,768]{1,0:T(8,128)(2,1)S(1)}, u32[]{:S(2)}, u32[]{:S(2)}) collective-permute-start(bf16[40,768]{1,0:T(8,128)(2,1)S(1)} %fusion.28), channel_id=1, source_target_pairs={{0,16},{8,24},{16,0},{24,8},{1,17},{9,25},{17,1},{25,9},{2,18},{10... | collective-permute-start | bytes 184328 | tf_op jit(solution)/shard_map/ppermute | solution.py:28
  48.2 2.6 %collective-permute-done.19 = bf16[40,768]{1,0:T(8,128)(2,1)S(1)} collective-permute-done((bf16[40,768]{1,0:T(8,128)(2,1)S(1)}, bf16[40,768]{1,0:T(8,128)(2,1)S(1)}, u32[]{:S(2)}, u32[]{:S(2)}) %collective-permute-start.19) | collective-permute-done | bytes 61472 | tf_op jit(solution)/shard_map/ppermute | solution.py:28
  50.9 1.3 %collective-permute-done.20 = bf16[80,768]{1,0:T(8,128)(2,1)S(1)} collective-permute-done((bf16[80,768]{1,0:T(8,128)(2,1)S(1)}, bf16[80,768]{1,0:T(8,128)(2,1)S(1)}, u32[]{:S(2)}, u32[]{:S(2)}) %collective-permute-start.20) | collective-permute-done | bytes 122912 | tf_op jit(solution)/shard_map/ppermute | solution.py:28
  52.3 1.6 %adam.1 = (f32[32,768]{1,0:T(8,128)}, f32[32,768]{1,0:T(8,128)}, f32[32,768]{1,0:T(8,128)}, f32[128,768]{1,0:T(8,128)}, f32[128,768]{1,0:T(8,128)}, /*index=5*/f32[128,768]{1,0:T(8,128)}) custom-call(bf16[160,768]{1,0:T(8,128)(2,1)S(1)} %pad_maximum_fusion.3.refs_0_, f32[32,768]{1,0:T(8,128)S(1)} %copy-done.4, f32[32,768]{1,0:T(8,128)S(1)} %copy-done.5, ...), custom_call_target="tpu_custom_call" | custom-call | tf_op jit(solution)/shard_map/adam/pallas_call | solution.py:362
  53.9 3.8 %collective-permute-done.13 = bf16[256,768]{1,0:T(8,128)(2,1)S(1)} collective-permute-done((bf16[256,768]{1,0:T(8,128)(2,1)S(1)}, bf16[256,768]{1,0:T(8,128)(2,1)S(1)}, u32[]{:S(2)}, u32[]{:S(2)}) %collective-permute-start.13) | collective-permute-done | bytes 393248 | tf_op jit(solution)/shard_map/ppermute | solution.py:28
  57.7 0.8 %fusion.12 = bf16[256,768]{1,0:T(8,128)(2,1)} fusion(f32[512,768]{1,0:T(8,128)S(1)} %convert_add_fusion, bf16[256,768]{1,0:T(8,128)(2,1)S(1)} %collective-permute-done.13), kind=kLoop, calls=%fused_computation.22 | loop fusion | flops 589824 | bytes 1572864 | tf_op jit(solution)/shard_map/convert_element_type | solution.py:358
  (62 shorter events, 6.7 us)
Async XLA Ops:
  0.6 25.6 %collective-permute-start.9 = (bf16[256,768]{1,0:T(8,128)(2,1)}, bf16[256,768]{1,0:T(8,128)(2,1)S(1)}, u32[]{:S(2)}, u32[]{:S(2)}) collective-permute-start(bf16[256,768]{1,0:T(8,128)(2,1)} %in_ref.1), channel_id=1, source_target_pairs={{0,16},{8,24},{16,0},{24,8},{1,17},{9,25},{17,1},{25,9},{2,18},{10... | collective-permute-start | bytes 1179656 | tf_op jit(solution)/shard_map/ppermute | solution.py:28
  4.9 8.6 %collective-permute-start = (bf16[16,768]{1,0:T(8,128)(2,1)S(1)}, bf16[16,768]{1,0:T(8,128)(2,1)S(1)}, u32[]{:S(2)}, u32[]{:S(2)}) collective-permute-start(bf16[16,768]{1,0:T(8,128)(2,1)S(1)} %get-tuple-element.22), channel_id=1, source_target_pairs={{0,16},{8,24},{16,0},{24,8},{1,17},{9,25},{17,1},{25,9},{2,18},{10... | collective-permute-start | bytes 73736 | tf_op jit(solution)/shard_map/ppermute | solution.py:28
  5.0 25.2 %collective-permute-start.8 = (bf16[40,768]{1,0:T(8,128)(2,1)S(1)}, bf16[40,768]{1,0:T(8,128)(2,1)S(1)}, u32[]{:S(2)}, u32[]{:S(2)}) collective-permute-start(bf16[40,768]{1,0:T(8,128)(2,1)S(1)} %get-tuple-element.24), channel_id=1, source_target_pairs={{0,1},{1,0},{2,3},{3,2},{4,5},{5,4},{6,7},{7,6},{8,9},{9,8},{10,11... | collective-permute-start | bytes 184328 | tf_op jit(solution)/shard_map/ppermute | solution.py:28
  7.0 10.3 %collective-permute-start.6 = (bf16[40,768]{1,0:T(8,128)(2,1)S(1)}, bf16[40,768]{1,0:T(8,128)(2,1)S(1)}, u32[]{:S(2)}, u32[]{:S(2)}) collective-permute-start(bf16[40,768]{1,0:T(8,128)(2,1)S(1)} %get-tuple-element.24), channel_id=1, source_target_pairs={{0,2},{1,3},{2,0},{3,1},{4,6},{5,7},{6,4},{7,5},{8,10},{9,11},{10,... | collective-permute-start | bytes 184328 | tf_op jit(solution)/shard_map/ppermute | solution.py:28
  8.6 8.8 %collective-permute-start.4 = (bf16[40,768]{1,0:T(8,128)(2,1)S(1)}, bf16[40,768]{1,0:T(8,128)(2,1)S(1)}, u32[]{:S(2)}, u32[]{:S(2)}) collective-permute-start(bf16[40,768]{1,0:T(8,128)(2,1)S(1)} %get-tuple-element.24), channel_id=1, source_target_pairs={{0,4},{1,5},{2,6},{3,7},{4,0},{5,1},{6,2},{7,3},{8,12},{9,13},{10,... | collective-permute-start | bytes 184328 | tf_op jit(solution)/shard_map/ppermute | solution.py:28
  13.5 6.1 %collective-permute-start.2 = (bf16[40,768]{1,0:T(8,128)(2,1)S(1)}, bf16[40,768]{1,0:T(8,128)(2,1)S(1)}, u32[]{:S(2)}, u32[]{:S(2)}) collective-permute-start(bf16[40,768]{1,0:T(8,128)(2,1)S(1)} %get-tuple-element.24), channel_id=1, source_target_pairs={{0,6},{1,7},{2,4},{3,5},{4,2},{5,3},{6,0},{7,1},{8,14},{9,15},{10,... | collective-permute-start | bytes 184328 | tf_op jit(solution)/shard_map/ppermute | solution.py:28
  17.4 12.9 %collective-permute-start.10 = (bf16[256,768]{1,0:T(8,128)(2,1)}, bf16[256,768]{1,0:T(8,128)(2,1)S(1)}, u32[]{:S(2)}, u32[]{:S(2)}) collective-permute-start(bf16[256,768]{1,0:T(8,128)(2,1)} %in_ref.1), channel_id=1, source_target_pairs={{0,8},{8,0},{16,24},{24,16},{1,9},{9,1},{17,25},{25,17},{2,10},{10... | collective-permute-start | bytes 1179656 | tf_op jit(solution)/shard_map/ppermute | solution.py:28
  17.5 3.9 %collective-permute-start.1 = (bf16[32,768]{1,0:T(8,128)(2,1)S(1)}, bf16[32,768]{1,0:T(8,128)(2,1)S(1)}, u32[]{:S(2)}, u32[]{:S(2)}) collective-permute-start(bf16[32,768]{1,0:T(8,128)(2,1)S(1)} %pad_maximum_fusion.6), channel_id=1, source_target_pairs={{0,8},{8,0},{16,24},{24,16},{1,9},{9,1},{17,25},{25,17},{2,10},{10... | collective-permute-start | bytes 147464 | tf_op jit(solution)/shard_map/ppermute | solution.py:28
  19.7 10.6 %collective-permute-start.7 = (bf16[40,768]{1,0:T(8,128)(2,1)S(1)}, bf16[40,768]{1,0:T(8,128)(2,1)S(1)}, u32[]{:S(2)}, u32[]{:S(2)}) collective-permute-start(bf16[40,768]{1,0:T(8,128)(2,1)S(1)} %collective-permute-done.6), channel_id=1, source_target_pairs={{0,1},{1,0},{2,3},{3,2},{4,5},{5,4},{6,7},{7,6},{8,9},{9,8},{10,11... | collective-permute-start | bytes 184328 | tf_op jit(solution)/shard_map/ppermute | solution.py:28
  21.3 4.7 %collective-permute-start.3 = (bf16[40,768]{1,0:T(8,128)(2,1)S(1)}, bf16[40,768]{1,0:T(8,128)(2,1)S(1)}, u32[]{:S(2)}, u32[]{:S(2)}) collective-permute-start(bf16[40,768]{1,0:T(8,128)(2,1)S(1)} %collective-permute-done.2), channel_id=1, source_target_pairs={{0,1},{1,0},{2,3},{3,2},{4,5},{5,4},{6,7},{7,6},{8,9},{9,8},{10,11... | collective-permute-start | bytes 184328 | tf_op jit(solution)/shard_map/ppermute | solution.py:28
  26.0 4.2 %collective-permute-start.5 = (bf16[40,768]{1,0:T(8,128)(2,1)S(1)}, bf16[40,768]{1,0:T(8,128)(2,1)S(1)}, u32[]{:S(2)}, u32[]{:S(2)}) collective-permute-start(bf16[40,768]{1,0:T(8,128)(2,1)S(1)} %collective-permute-done.4), channel_id=1, source_target_pairs={{0,1},{1,0},{2,3},{3,2},{4,5},{5,4},{6,7},{7,6},{8,9},{9,8},{10,11... | collective-permute-start | bytes 184328 | tf_op jit(solution)/shard_map/ppermute | solution.py:28
  26.2 4.1 %collective-permute-start.11 = (bf16[256,768]{1,0:T(8,128)(2,1)S(1)}, bf16[256,768]{1,0:T(8,128)(2,1)S(1)}, u32[]{:S(2)}, u32[]{:S(2)}) collective-permute-start(bf16[256,768]{1,0:T(8,128)(2,1)S(1)} %collective-permute-done.9), channel_id=1, source_target_pairs={{0,8},{8,0},{16,24},{24,16},{1,9},{9,1},{17,25},{25,17},{2,10},{10... | collective-permute-start | bytes 1179656 | tf_op jit(solution)/shard_map/ppermute | solution.py:28
  31.5 4.9 %collective-permute-start.15 = (bf16[80,768]{1,0:T(8,128)(2,1)S(1)}, bf16[80,768]{1,0:T(8,128)(2,1)S(1)}, u32[]{:S(2)}, u32[]{:S(2)}) collective-permute-start(bf16[80,768]{1,0:T(8,128)(2,1)S(1)} %get-tuple-element.39), channel_id=1, source_target_pairs={{0,1},{1,0},{2,3},{3,2},{4,5},{5,4},{6,7},{7,6},{8,9},{9,8},{10,11... | collective-permute-start | bytes 368648 | tf_op jit(solution)/shard_map/ppermute | solution.py:28
  31.8 8.5 %collective-permute-start.14 = (bf16[80,768]{1,0:T(8,128)(2,1)S(1)}, bf16[80,768]{1,0:T(8,128)(2,1)S(1)}, u32[]{:S(2)}, u32[]{:S(2)}) collective-permute-start(bf16[80,768]{1,0:T(8,128)(2,1)S(1)} %get-tuple-element.40), channel_id=1, source_target_pairs={{0,1},{1,0},{2,3},{3,2},{4,5},{5,4},{6,7},{7,6},{8,9},{9,8},{10,11... | collective-permute-start | bytes 368648 | tf_op jit(solution)/shard_map/ppermute | solution.py:28
  35.0 12.4 %collective-permute-start.12 = (bf16[512,768]{1,0:T(8,128)(2,1)S(1)}, bf16[512,768]{1,0:T(8,128)(2,1)S(1)}, u32[]{:S(2)}, u32[]{:S(2)}) collective-permute-start(bf16[512,768]{1,0:T(8,128)(2,1)S(1)} %convolution_convert_fusion.1), channel_id=1, source_target_pairs={{0,8},{8,0},{16,24},{24,16},{1,9},{9,1},{17,25},{25,17},{2,10},{10... | collective-permute-start | bytes 2359304 | tf_op jit(solution)/shard_map/ppermute | solution.py:28
  36.5 6.2 %collective-permute-start.16 = (bf16[40,768]{1,0:T(8,128)(2,1)S(1)}, bf16[40,768]{1,0:T(8,128)(2,1)S(1)}, u32[]{:S(2)}, u32[]{:S(2)}) collective-permute-start(bf16[40,768]{1,0:T(8,128)(2,1)S(1)} %slice_add_fusion.4), channel_id=1, source_target_pairs={{0,6},{1,7},{2,4},{3,5},{4,2},{5,3},{6,0},{7,1},{8,14},{9,15},{10,... | collective-permute-start | bytes 184328 | tf_op jit(solution)/shard_map/ppermute | solution.py:28
  40.3 5.2 %collective-permute-start.17 = (bf16[40,768]{1,0:T(8,128)(2,1)S(1)}, bf16[40,768]{1,0:T(8,128)(2,1)S(1)}, u32[]{:S(2)}, u32[]{:S(2)}) collective-permute-start(bf16[40,768]{1,0:T(8,128)(2,1)S(1)} %get-tuple-element.37), channel_id=1, source_target_pairs={{0,4},{1,5},{2,6},{3,7},{4,0},{5,1},{6,2},{7,3},{8,12},{9,13},{10,... | collective-permute-start | bytes 184328 | tf_op jit(solution)/shard_map/ppermute | solution.py:28
  40.4 5.4 %collective-permute-start.18 = (bf16[40,768]{1,0:T(8,128)(2,1)S(1)}, bf16[40,768]{1,0:T(8,128)(2,1)S(1)}, u32[]{:S(2)}, u32[]{:S(2)}) collective-permute-start(bf16[40,768]{1,0:T(8,128)(2,1)S(1)} %get-tuple-element.38), channel_id=1, source_target_pairs={{0,2},{1,3},{2,0},{3,1},{4,6},{5,7},{6,4},{7,5},{8,10},{9,11},{10,... | collective-permute-start | bytes 184328 | tf_op jit(solution)/shard_map/ppermute | solution.py:28
  45.8 6.5 %copy-start = (f32[128,768]{1,0:T(8,128)S(1)}, f32[128,768]{1,0:T(8,128)}, u32[]{:S(2)}) copy-start(f32[128,768]{1,0:T(8,128)} %refs_4_.1) | copy-start | bytes 1179652
  45.8 6.4 %copy-start.2 = (f32[128,768]{1,0:T(8,128)S(1)}, f32[128,768]{1,0:T(8,128)}, u32[]{:S(2)}) copy-start(f32[128,768]{1,0:T(8,128)} %refs_5_.1) | copy-start | bytes 1179652
  45.8 6.4 %copy-start.3 = (f32[128,768]{1,0:T(8,128)S(1)}, f32[128,768]{1,0:T(8,128)}, u32[]{:S(2)}) copy-start(f32[128,768]{1,0:T(8,128)} %refs_6_.3) | copy-start | bytes 1179652
  45.9 4.9 %collective-permute-start.19 = (bf16[40,768]{1,0:T(8,128)(2,1)S(1)}, bf16[40,768]{1,0:T(8,128)(2,1)S(1)}, u32[]{:S(2)}, u32[]{:S(2)}) collective-permute-start(bf16[40,768]{1,0:T(8,128)(2,1)S(1)} %fusion.28), channel_id=1, source_target_pairs={{0,16},{8,24},{16,0},{24,8},{1,17},{9,25},{17,1},{25,9},{2,18},{10... | collective-permute-start | bytes 184328 | tf_op jit(solution)/shard_map/ppermute | solution.py:28
  47.6 10.0 %collective-permute-start.13 = (bf16[256,768]{1,0:T(8,128)(2,1)S(1)}, bf16[256,768]{1,0:T(8,128)(2,1)S(1)}, u32[]{:S(2)}, u32[]{:S(2)}) collective-permute-start(bf16[256,768]{1,0:T(8,128)(2,1)S(1)} %slice.123), channel_id=1, source_target_pairs={{0,16},{8,24},{16,0},{24,8},{1,17},{9,25},{17,1},{25,9},{2,18},{10... | collective-permute-start | bytes 1179656 | tf_op jit(solution)/shard_map/ppermute | solution.py:28
  50.8 1.4 %collective-permute-start.20 = (bf16[80,768]{1,0:T(8,128)(2,1)S(1)}, bf16[80,768]{1,0:T(8,128)(2,1)S(1)}, u32[]{:S(2)}, u32[]{:S(2)}) collective-permute-start(bf16[80,768]{1,0:T(8,128)(2,1)S(1)} %pad_maximum_fusion.4), channel_id=1, source_target_pairs={{0,8},{8,0},{16,24},{24,16},{1,9},{9,1},{17,25},{25,17},{2,10},{10... | collective-permute-start | bytes 368648 | tf_op jit(solution)/shard_map/ppermute | solution.py:28
  (4 other events, 20.3 us)
